TPU v7x, 32 devices: a whole 2x2x4 slice. The times are simulated.
32 devices in a mesh: cube: 2 (over y), row: 4 (over x, core), col: 4 (over z).
Axes of the slice: x: 2, y: 2, z: 4, core: 2. Of those that a mesh axis runs over, the one named last changes fastest.
Arguments:
- child_panel: bfloat16 [2, 6144, 256], P('cube', ('row', 'col')), may hold values from -0.75 to 0.75
- child_inverse: float32 [2, 256, 256], P('cube')
- child_trailing: bfloat16 [2, 6144, 6144], P('cube', ('row', 'col')), may hold values from -6 to 6
- child_pattern: int32 [2, 48], P('cube'), may hold values 0 or 1
- child_map: int32 [2, 48], replicated, may hold values from 0 to 95, as said below
- parent_panel: bfloat16 [2, 6144, 256], P('cube', ('row', 'col')), may hold values from -0.75 to 0.75
- parent_inverse: float32 [1, 256, 256], replicated
- parent_trailing: bfloat16 [2, 6144, 12288], P('cube', ('row', 'col')), may hold values from -6 to 6
- parent_pattern: int32 [1, 96], replicated, may hold values 0 or 1
Outputs:
- parent_update: bfloat16 [2, 6144, 12288], P('cube', ('row', 'col'))
Inputs may be any that keep to these rules, and one draw needn't show every extreme that they name: With p = i // 3, child_map[c, i] is one of the blocks h * 48 + p * 3 + k, h in 0 and 1, k from 0 to 2; a child's blocks land on distinct parent blocks.
All inputs are finite; a program needn't handle non-finite values. No bound on the sum of `child_pattern` on one device may be relied on, other than what follows from the above.
Results may differ from a plain program's by a relative error of at most 0.0042.
Values may be sent and summed in bfloat16 or wider, within the bound.
No kernel may reach another device: no remote copies, remote signals or barrier semaphores. Data moves between devices by JAX's collectives and lax.ppermute only.
A program may use at most 192 MiB of HBM per device.

v0:
```python
import jax
import jax.numpy as jnp
from jax import lax
from jax.sharding import PartitionSpec as P

BLOCK = 128


def from_partner(array, axis, apart):
    return lax.ppermute(array, axis, [(i, i ^ 1 << apart) for i in range(lax.axis_size(axis))])


def row_mask(pattern_row, start, how_many):
    window = lax.dynamic_slice_in_dim(pattern_row, start, how_many)
    return jnp.repeat(window, BLOCK).astype(jnp.bfloat16)[:, None]


def one_hot(mapping, extent):
    return (mapping[:, None] == jnp.arange(extent, dtype=jnp.int32)[None, :]).astype(jnp.bfloat16)


def map_columns(values, table):
    row_count = values.shape[0]
    blocks = values.reshape(row_count, table.shape[0], BLOCK)
    shifted = jnp.einsum("rib,ip->rpb", blocks, table, preferred_element_type=jnp.float32)
    return shifted.reshape(row_count, table.shape[1] * BLOCK)


def map_rows(values, table):
    column_count = values.shape[1]
    blocks = values.reshape(table.shape[0], BLOCK, column_count)
    shifted = jnp.einsum("iaw,ip->paw", blocks, table, preferred_element_type=jnp.float32)
    return shifted.reshape(table.shape[1] * BLOCK, column_count)


def contribution(trailing, own_panel, whole_panel, inverse):
    left_factor = jnp.dot(
        own_panel.astype(jnp.float32), inverse, precision=lax.Precision.HIGHEST
    ).astype(jnp.bfloat16)
    update = lax.dot_general(
        left_factor, whole_panel, (((1,), (1,)), ((), ())), preferred_element_type=jnp.float32
    )
    return trailing.astype(jnp.float32) - update


def local(
    child_panel,
    child_inverse,
    child_trailing,
    child_pattern,
    child_map,
    parent_panel,
    parent_inverse,
    parent_trailing,
    parent_pattern,
):
    position = lax.axis_index(("row", "col"))
    cube_index = lax.axis_index("cube")
    half_bit = cube_index % 2
    parent = cube_index // 2
    parent_blocks = parent_pattern.shape[1]
    half_rows = parent_trailing.shape[1] * lax.axis_size(("row", "col"))
    panel_piece = child_panel[0]
    blocks_here = panel_piece.shape[0] // BLOCK
    own_panel = panel_piece * row_mask(child_pattern[0], position * blocks_here, blocks_here)
    whole_panel = lax.all_gather(own_panel, ("row", "col"), axis=0, tiled=True)
    schur_rows = contribution(child_trailing[0], own_panel, whole_panel, child_inverse[0]).astype(
        jnp.bfloat16
    )
    own_map = lax.dynamic_index_in_dim(child_map, cube_index, 0, keepdims=False)
    own_table = one_hot(own_map, parent_blocks)
    widened = map_columns(schur_rows, own_table).astype(jnp.bfloat16)
    spread = lax.all_to_all(widened, ("row", "col"), split_axis=1, concat_axis=0, tiled=True)
    placed = map_rows(spread, own_table).astype(jnp.bfloat16)
    own_half = lax.dynamic_slice_in_dim(placed, half_bit * half_rows, half_rows, 0)
    theirs = lax.dynamic_slice_in_dim(placed, (1 - half_bit) * half_rows, half_rows, 0)
    arrived = from_partner(theirs, "cube", 0)
    summed = (own_half.astype(jnp.float32) + arrived.astype(jnp.float32)).astype(jnp.bfloat16)
    assembled = lax.all_to_all(summed, ("row", "col"), split_axis=0, concat_axis=1, tiled=True)
    parent_piece = parent_panel[0]
    parent_here = parent_piece.shape[0] // BLOCK
    pattern_row = lax.dynamic_index_in_dim(parent_pattern, parent, 0, keepdims=False)
    own_parent = parent_piece * row_mask(
        pattern_row, half_bit * (half_rows // BLOCK) + position * parent_here, parent_here
    )
    half_panel = lax.all_gather(own_parent, ("row", "col"), axis=0, tiled=True)
    other_panel = from_partner(half_panel, "cube", 0)
    whole_parent = jnp.where(
        half_bit == 0,
        jnp.concatenate([half_panel, other_panel], axis=0),
        jnp.concatenate([other_panel, half_panel], axis=0),
    )
    inverse = lax.dynamic_index_in_dim(parent_inverse, parent, 0, keepdims=False)
    result = contribution(parent_trailing[0], own_parent, whole_parent, inverse) + assembled.astype(
        jnp.float32
    )
    return result.astype(jnp.bfloat16)[None]


def solution(mesh):
    in_specs = (
        P("cube", ("row", "col"), None),
        P("cube", None, None),
        P("cube", ("row", "col"), None),
        P("cube", None),
        P(),
        P("cube", ("row", "col"), None),
        P(),
        P("cube", ("row", "col"), None),
        P(),
    )
    out_specs = P("cube", ("row", "col"), None)
    return jax.shard_map(local, mesh=mesh, in_specs=in_specs, out_specs=out_specs, check_vma=False)
```

profile of v0, /device:TPU:0, one launch (start us, length us, event | category | flops | bytes accessed | tf_op | source)
XLA Modules:
  0.0 852.1 jit_solution(2174740888799487291)
XLA Ops:
  6.5 0.0 copy-start
  6.5 0.0 all-gather.5.cloned.1.call-start
  6.5 0.8 fusion.29
  7.3 0.1 broadcast_bitcast_fusion
  7.4 1.7 bitcast_multiply_fusion
  9.1 0.0 all-gather.5.cloned.1.call-update
  9.1 0.7 fusion.27
  9.8 0.0 copy-done
  9.8 1.3 convolution_convert_fusion.1
  11.1 46.5 %all-gather.5.cloned.1.call-done = bf16[6144,256]{1,0:T(8,128)(2,1)} async-done(((bf16[384,256]{1,0:T(8,128)(2,1)}), bf16[6144,256]{1,0:T(8,128)(2,1)}) %all-gather.5.cloned.1.call-update) | async-done | bytes 3145744 | tf_op jit(solution)/shard_map/all_gather | solution.py:66
  57.6 4.7 fusion.11
  62.3 1.3 copy.15
  63.6 5.2 convert_bitcast_fusion.1
  68.8 16.8 %convert_element_type.104 = bf16[384,16,768]{2,1,0:T(8,128)(2,1)} reshape(bf16[384,96,128]{2,1,0:T(8,128)(2,1)} %convert_bitcast_fusion.1) | data formatting | bytes 18874368 | tf_op jit(solution)/shard_map/convert_element_type | solution.py:72
  85.6 10.7 %copy.10 = bf16[384,16,768]{2,0,1:T(8,128)(2,1)} copy(bf16[384,16,768]{2,1,0:T(8,128)(2,1)} %convert_element_type.104) | data formatting | bytes 18874368 | tf_op jit(solution)/shard_map/convert_element_type | solution.py:72
  96.3 5.0 all-to-all-start
  101.3 206.5 %all-to-all-done = bf16[384,16,768]{2,0,1:T(8,128)(2,1)} async-done(((bf16[384,16,768]{2,0,1:T(8,128)(2,1)}), bf16[384,16,768]{2,0,1:T(8,128)(2,1)}, u32[]{:S(2)}, u32[]{:S(2)}) %all-to-all-start) | async-done | bytes 9437216 | tf_op jit(solution)/shard_map/all_to_all | solution.py:73
  307.9 16.0 %convolution_convert_fusion = bf16[96,128,768]{2,0,1:T(8,128)(2,1)} fusion(bf16[48,128,768]{2,1,0:T(8,128)(2,1)} %bitcast.16, s32[48]{0:T(128)S(1)} %fusion.27), kind=kOutput, calls=%fused_computation.6 | convolution fusion | flops 915411456 | bytes 28311744 | tf_op jit(solution)/shard_map/iaw,ip->paw/dot_general | solution.py:32
  323.9 20.2 %copy.12 = bf16[96,128,768]{2,1,0:T(8,128)(2,1)} copy(bf16[96,128,768]{2,0,1:T(8,128)(2,1)} %convolution_convert_fusion) | data formatting | bytes 37748736 | tf_op jit(solution)/shard_map/convert_element_type | solution.py:74
  344.1 8.0 constant_dynamic-slice_fusion
  352.1 1.5 collective-permute-start.1
  353.7 203.2 %collective-permute-done.1 = bf16[6144,768]{1,0:T(8,128)(2,1)} collective-permute-done((bf16[6144,768]{1,0:T(8,128)(2,1)}, bf16[6144,768]{1,0:T(8,128)(2,1)}, u32[]{:S(2)}, u32[]{:S(2)}) %collective-permute-start.1) | collective-permute-done | bytes 9437216 | tf_op jit(solution)/shard_map/ppermute | solution.py:10
  556.9 11.9 %add_convert_fusion = bf16[6144,768]{1,0:T(8,128)(2,1)} fusion(bf16[6144,768]{1,0:T(8,128)(2,1)} %collective-permute-done.1, bf16[12288,768]{1,0:T(8,128)(2,1)} %bitcast.60, s32[]{:T(128)S(6)} %select_n.43), kind=kLoop, calls=%fused_computation.4 | loop fusion | flops 18874368 | bytes 28311556 | tf_op jit(solution)/shard_map/convert_element_type | solution.py:78
  568.8 0.0 copy-start.5
  568.8 0.0 copy-start.3
  568.8 0.0 copy-start.4
  568.8 4.9 all-to-all-start.1
  573.8 0.3 all-gather.3.cloned.1.call-start
  574.1 0.0 copy-done.5
  574.1 0.1 fusion.26
  574.1 0.1 broadcast_bitcast_fusion.1
  574.2 0.0 copy-done.3
  574.2 0.8 bitcast_multiply_fusion.1
  575.0 0.0 all-gather.3.cloned.1.call-update
  575.1 157.3 %all-gather.3.cloned.1.call-done = bf16[6144,256]{1,0:T(8,128)(2,1)} async-done(((bf16[384,256]{1,0:T(8,128)(2,1)}), bf16[6144,256]{1,0:T(8,128)(2,1)}) %all-gather.3.cloned.1.call-update) | async-done | bytes 3145744 | tf_op jit(solution)/shard_map/all_gather | solution.py:86
  732.4 1.5 collective-permute-start
  733.9 0.0 copy-done.4
  733.9 1.0 convolution_convert_fusion.2
  734.9 64.5 %all-to-all-done.1 = bf16[16,384,768]{2,1,0:T(8,128)(2,1)} async-done(((bf16[16,384,768]{2,1,0:T(8,128)(2,1)}), bf16[16,384,768]{2,1,0:T(8,128)(2,1)}, u32[]{:S(2)}, u32[]{:S(2)}) %all-to-all-start.1) | async-done | bytes 9437216 | tf_op jit(solution)/shard_map/all_to_all | solution.py:79
  799.5 12.2 %convert_bitcast_fusion = f32[16,48,8,768]{3,2,1,0:T(8,128)} fusion(bf16[16,384,768]{2,1,0:T(8,128)(2,1)} %all-to-all-done.1), kind=kLoop, calls=%fused_computation.3 | loop fusion | flops 4718592 | bytes 28311552
  811.7 0.0 copy-start.2
  811.7 12.9 %copy.14 = f32[16,48,8,768]{3,2,0,1:T(8,128)} copy(f32[16,48,8,768]{3,2,1,0:T(8,128)} %convert_bitcast_fusion) | data formatting | bytes 37748736 | tf_op jit(solution)/shard_map/convert_element_type | solution.py:94
  824.6 0.0 collective-permute-done
  824.6 0.0 copy-done.2
  824.6 0.0 copy-start.1
  824.6 20.6 %fusion.2 = bf16[1,384,12288]{2,1,0:T(8,128)(2,1)} fusion(f32[384,12288]{1,0:T(8,128)} %bitcast.58, bf16[384,256]{1,0:T(8,128)(2,1)} %convolution_convert_fusion.2, bf16[1,384,12288]{2,1,0:T(8,128)(2,1)} %param.16, bf16[6144,256]{1,0:T(8,128)(2,1)} %collective-permute-done, bf16[6144,256]{1,0:T(8,128)(2,1)S(1)} %copy-done.2, pred[]{:T(512)S(6)} %eq.20), kind=kOutput, calls=%fused_computation.5 | convolution fusion | flops 2463105024 | bytes 44236800 | tf_op jit(solution)/shard_map/dot_general | solution.py:40
  845.2 0.0 copy-done.1
Async XLA Ops:
  6.5 3.3 copy-start
  6.5 51.0 %all-gather.5.cloned.1.call-start = ((), (), s32[]{:S(2)}) async-start(), calls=%async_computation.3 | async-start | bytes 3342336 | tf_op jit(solution)/shard_map/all_gather | solution.py:66
  96.3 211.5 %all-to-all-start = ((bf16[384,16,768]{2,0,1:T(8,128)(2,1)}), bf16[384,16,768]{2,0,1:T(8,128)(2,1)}, u32[]{:S(2)}, u32[]{:S(2)}) async-start(bf16[384,16,768]{2,0,1:T(8,128)(2,1)} %copy.10), calls=%async_computation | async-start | bytes 18874368 | tf_op jit(solution)/shard_map/all_to_all | solution.py:73
  352.1 204.8 %collective-permute-start.1 = (bf16[6144,768]{1,0:T(8,128)(2,1)}, bf16[6144,768]{1,0:T(8,128)(2,1)}, u32[]{:S(2)}, u32[]{:S(2)}) collective-permute-start(bf16[6144,768]{1,0:T(8,128)(2,1)} %constant_dynamic-slice_fusion), channel_id=1, source_target_pairs={{0,16},{16,0},{1,17},{17,1},{2,18},{18,2},{3,19},{19,3},{4,20},{20... | collective-permute-start | bytes 28311560 | tf_op jit(solution)/shard_map/ppermute | solution.py:10
  568.8 5.2 copy-start.5
  568.8 5.4 copy-start.3
  568.8 165.1 %copy-start.4 = (f32[1,256,256]{2,1,0:T(8,128)S(1)}, f32[1,256,256]{2,1,0:T(8,128)}, u32[]{:S(2)}) copy-start(f32[1,256,256]{2,1,0:T(8,128)} %param.15) | copy-start | bytes 786436
  568.8 230.6 %all-to-all-start.1 = ((bf16[16,384,768]{2,1,0:T(8,128)(2,1)}), bf16[16,384,768]{2,1,0:T(8,128)(2,1)}, u32[]{:S(2)}, u32[]{:S(2)}) async-start(bf16[16,384,768]{2,1,0:T(8,128)(2,1)} %bitcast.61), calls=%async_computation.1 | async-start | bytes 18874368 | tf_op jit(solution)/shard_map/all_to_all | solution.py:79
  573.8 158.6 %all-gather.3.cloned.1.call-start = ((), (), s32[]{:S(2)}) async-start(), calls=%async_computation.2 | async-start | bytes 3342336 | tf_op jit(solution)/shard_map/all_gather | solution.py:86
  732.4 92.2 %collective-permute-start = (bf16[6144,256]{1,0:T(8,128)(2,1)}, bf16[6144,256]{1,0:T(8,128)(2,1)}, u32[]{:S(2)}, u32[]{:S(2)}) collective-permute-start(bf16[6144,256]{1,0:T(8,128)(2,1)} %all-gather.3.cloned.1.call-done), channel_id=1, source_target_pairs={{0,16},{16,0},{1,17},{17,1},{2,18},{18,2},{3,19},{19,3},{4,20},{20... | collective-permute-start | bytes 9437192 | tf_op jit(solution)/shard_map/ppermute | solution.py:10
  811.7 12.9 %copy-start.2 = (bf16[6144,256]{1,0:T(8,128)(2,1)S(1)}, bf16[6144,256]{1,0:T(8,128)(2,1)}, u32[]{:S(2)}) copy-start(bf16[6144,256]{1,0:T(8,128)(2,1)} %all-gather.3.cloned.1.call-done) | copy-start | bytes 9437188
  824.6 20.6 %copy-start.1 = (f32[1,256,256]{2,1,0:T(8,128)S(1)}, f32[1,256,256]{2,1,0:T(8,128)}, u32[]{:S(2)}) copy-start(f32[1,256,256]{2,1,0:T(8,128)} %param.10) | copy-start | bytes 786436
Sparse Core Ops, SparseCore 0:
  9.7 47.8 all-gather.4
  576.9 155.3 all-gather.2
where the time goes:
time: 853 us; the launch traced here: 852 us
  waiting for transfers between devices  678 us (79%)
  local copies, waits for them, and re-layouts  70.8 us (8%)
  matrix products  48.9 us (6%)
  other arithmetic  27.5 us (3%)
  between operations  13.5 us (2%)
  starting transfers between devices  13.2 us (2%)
    all_to_all x1, waiting for transfers between devices, local(): lax.all_to_all(widened, ('row', 'col'), split_axis=1, concat_axis=0, tile...  207 us
    ppermute x2, waiting for transfers between devices, from_partner(): lax.ppermute(array, axis, [(i, i ^ 1 << apart) for i in range(lax.axis_si...  203 us
    all_gather x1, waiting for transfers between devices, local(): half_panel = lax.all_gather(own_parent, ('row', 'col'), axis=0, tiled=True)  157 us
    all_to_all x1, waiting for transfers between devices, local(): lax.all_to_all(summed, ('row', 'col'), split_axis=0, concat_axis=1, tiled...  64.5 us
    all_gather x1, waiting for transfers between devices, local(): whole_panel = lax.all_gather(own_panel, ('row', 'col'), axis=0, tiled=True)  46.5 us
    convert_element_type x2, local copies, waits for them, and re-layouts, local(): widened = map_columns(schur_rows, own_table).astype(jnp.bfloat16)  27.5 us
    dot_general x2, matrix products, contribution(): lax.dot_general(left_factor, whole_panel, (((1,), (1,)), ((), ())), prefe...  25.3 us
    convert_element_type x1, local copies, waits for them, and re-layouts, local(): placed = map_rows(spread, own_table).astype(jnp.bfloat16)  20.2 us
  transfers between devices with their start and end apart: 6, of which 5 were waited for; matrix products, arithmetic and copies ran while one was open for 3% of the time, Pallas kernels for 0%

commit v1 on v0

--- a/solution.py
+++ b/solution.py
@@ -63,7 +63,30 @@
     panel_piece = child_panel[0]
     blocks_here = panel_piece.shape[0] // BLOCK
     own_panel = panel_piece * row_mask(child_pattern[0], position * blocks_here, blocks_here)
-    whole_panel = lax.all_gather(own_panel, ("row", "col"), axis=0, tiled=True)
+    ways, here, step = (
+        lax.axis_size(("row", "col")),
+        lax.axis_index(("row", "col")),
+        own_panel.shape[0],
+    )
+    shape = [n * ways if d == 0 else n for d, n in enumerate(own_panel.shape)]
+    whole_panel = lax.dynamic_update_slice_in_dim(
+        jnp.zeros(shape, own_panel.dtype), own_panel, here * step, axis=0
+    )
+    going_up = going_down = own_panel
+    for far in range(1, ways // 2 + 1):
+        going_up = lax.ppermute(
+            going_up, ("row", "col"), [(d, (d + 1) % ways) for d in range(ways)]
+        )
+        whole_panel = lax.dynamic_update_slice_in_dim(
+            whole_panel, going_up, (here - far) % ways * step, axis=0
+        )
+        if 2 * far < ways:
+            going_down = lax.ppermute(
+                going_down, ("row", "col"), [(d, (d - 1) % ways) for d in range(ways)]
+            )
+            whole_panel = lax.dynamic_update_slice_in_dim(
+                whole_panel, going_down, (here + far) % ways * step, axis=0
+            )
     schur_rows = contribution(child_trailing[0], own_panel, whole_panel, child_inverse[0]).astype(
         jnp.bfloat16
     )

time: 853 us -> 885 us (1.038)
  starting transfers between devices: 13.2 us -> 70.3 us
  waiting for transfers between devices: 678 us -> 653 us
    ppermute x0 -> x15, starting transfers between devices: none -> 55.7 us  [the longest x8 47.3 us: local(): lax.ppermute(going_up, ('row', 'col'), [(d, (d + 1) % ways) for d in rang...]
    all_gather x1 -> x0, waiting for transfers between devices: 46.5 us -> none  [local(): whole_panel = lax.all_gather(own_panel, ('row', 'col'), axis=0, tiled=True)]
    ppermute x0 -> x15, waiting for transfers between devices: none -> 21.4 us  [the longest x8 17.1 us: local(): lax.ppermute(going_up, ('row', 'col'), [(d, (d + 1) % ways) for d in rang...]
  transfers between devices with their start and end apart: 6 -> 20, of which waited for: 5 -> 14; matrix products, arithmetic and copies ran while one was open for 3% -> 4% of each run, Pallas kernels for 0% -> 0%
where the time goes in v1:
time: 885 us; the launch traced here: 884 us
  waiting for transfers between devices  653 us (74%)
  local copies, waits for them, and re-layouts  73.2 us (8%)
  starting transfers between devices  70.3 us (8%)
  matrix products  45.5 us (5%)
  other arithmetic  27.5 us (3%)
  between operations  13.6 us (2%)
    all_to_all x1, waiting for transfers between devices, local(): lax.all_to_all(widened, ('row', 'col'), split_axis=1, concat_axis=0, tile...  207 us
    ppermute x2, waiting for transfers between devices, from_partner(): lax.ppermute(array, axis, [(i, i ^ 1 << apart) for i in range(lax.axis_si...  203 us
    all_gather x1, waiting for transfers between devices, local(): half_panel = lax.all_gather(own_parent, ('row', 'col'), axis=0, tiled=True)  157 us
    all_to_all x1, waiting for transfers between devices, local(): lax.all_to_all(summed, ('row', 'col'), split_axis=0, concat_axis=1, tiled...  64.6 us
    ppermute x8, starting transfers between devices, local(): lax.ppermute(going_up, ('row', 'col'), [(d, (d + 1) % ways) for d in rang...  47.3 us
    convert_element_type x2, local copies, waits for them, and re-layouts, local(): widened = map_columns(schur_rows, own_table).astype(jnp.bfloat16)  27.5 us
    dot_general x2, matrix products, contribution(): lax.dot_general(left_factor, whole_panel, (((1,), (1,)), ((), ())), prefe...  22 us
    convert_element_type x1, local copies, waits for them, and re-layouts, local(): placed = map_rows(spread, own_table).astype(jnp.bfloat16)  20.1 us
  transfers between devices with their start and end apart: 20, of which 14 were waited for; matrix products, arithmetic and copies ran while one was open for 4% of the time, Pallas kernels for 0%

profile of v1, /device:TPU:0, one launch (start us, length us, event | category | flops | bytes accessed | tf_op | source)
XLA Modules:
  0.0 883.6 jit_solution(324860102933984802)
XLA Ops:
  6.5 0.8 fusion.29
  7.3 0.1 broadcast_bitcast_fusion
  7.4 0.2 broadcast_in_dim.18
  7.6 1.7 constant_dynamic-update-slice_fusion.15
  9.3 3.0 collective-permute-start.1
  12.3 2.4 collective-permute-start.2
  14.7 0.8 fusion.27
  15.6 1.5 convolution_convert_fusion.1
  17.1 2.8 collective-permute-done.1
  19.8 0.6 collective-permute-start.3
  20.5 2.8 collective-permute-done.2
  23.2 2.9 collective-permute-start.4
  26.1 0.9 constant_dynamic-update-slice_fusion.14
  27.0 0.9 constant_dynamic-update-slice_fusion.13
  28.0 0.0 collective-permute-done.3
  28.0 4.9 collective-permute-start.5
  32.9 0.9 collective-permute-done.4
  33.9 1.2 collective-permute-start.6
  35.1 1.2 collective-permute-done.5
  36.3 7.6 collective-permute-start.7
  43.9 0.6 collective-permute-done.6
  44.6 0.1 collective-permute-start.8
  44.7 2.4 collective-permute-done.7
  47.1 8.6 collective-permute-start.9
  55.7 0.0 collective-permute-done.8
  55.7 0.0 collective-permute-start.10
  55.8 3.1 collective-permute-done.9
  58.9 7.9 collective-permute-start.11
  66.8 0.0 collective-permute-done.10
  66.8 0.4 collective-permute-start.12
  67.3 2.7 collective-permute-done.11
  70.0 7.1 collective-permute-start.13
  77.1 1.4 collective-permute-start.14
  78.6 1.7 collective-permute-done.13
  80.3 7.5 collective-permute-start.15
  87.8 0.0 collective-permute-done.14
  87.9 3.1 collective-permute-done.15
  91.0 1.5 fusion.11
  92.5 1.3 copy.15
  93.8 5.2 convert_bitcast_fusion.1
  99.0 16.8 %convert_element_type.104 = bf16[384,16,768]{2,1,0:T(8,128)(2,1)} reshape(bf16[384,96,128]{2,1,0:T(8,128)(2,1)} %convert_bitcast_fusion.1) | data formatting | bytes 18874368 | tf_op jit(solution)/shard_map/convert_element_type | solution.py:95
  115.9 10.7 %copy.10 = bf16[384,16,768]{2,0,1:T(8,128)(2,1)} copy(bf16[384,16,768]{2,1,0:T(8,128)(2,1)} %convert_element_type.104) | data formatting | bytes 18874368 | tf_op jit(solution)/shard_map/convert_element_type | solution.py:95
  126.6 6.4 all-to-all-start
  133.0 206.8 %all-to-all-done = bf16[384,16,768]{2,0,1:T(8,128)(2,1)} async-done(((bf16[384,16,768]{2,0,1:T(8,128)(2,1)}), bf16[384,16,768]{2,0,1:T(8,128)(2,1)}, u32[]{:S(2)}, u32[]{:S(2)}) %all-to-all-start) | async-done | bytes 9437216 | tf_op jit(solution)/shard_map/all_to_all | solution.py:96
  339.7 15.8 %convolution_convert_fusion = bf16[96,128,768]{2,0,1:T(8,128)(2,1)} fusion(bf16[48,128,768]{2,1,0:T(8,128)(2,1)} %bitcast.16, s32[48]{0:T(128)S(1)} %fusion.27), kind=kOutput, calls=%fused_computation.6 | convolution fusion | flops 915411456 | bytes 28311744 | tf_op jit(solution)/shard_map/iaw,ip->paw/dot_general | solution.py:32
  355.6 20.1 %copy.12 = bf16[96,128,768]{2,1,0:T(8,128)(2,1)} copy(bf16[96,128,768]{2,0,1:T(8,128)(2,1)} %convolution_convert_fusion) | data formatting | bytes 37748736 | tf_op jit(solution)/shard_map/convert_element_type | solution.py:97
  375.7 8.0 constant_dynamic-slice_fusion
  383.7 1.5 collective-permute-start.16
  385.2 203.3 %collective-permute-done.16 = bf16[6144,768]{1,0:T(8,128)(2,1)} collective-permute-done((bf16[6144,768]{1,0:T(8,128)(2,1)}, bf16[6144,768]{1,0:T(8,128)(2,1)}, u32[]{:S(2)}, u32[]{:S(2)}) %collective-permute-start.16) | collective-permute-done | bytes 9437216 | tf_op jit(solution)/shard_map/ppermute | solution.py:10
  588.5 11.9 %add_convert_fusion = bf16[6144,768]{1,0:T(8,128)(2,1)} fusion(bf16[6144,768]{1,0:T(8,128)(2,1)} %collective-permute-done.16, bf16[12288,768]{1,0:T(8,128)(2,1)} %bitcast.61, s32[]{:T(128)S(6)} %select_n.182), kind=kLoop, calls=%fused_computation.4 | loop fusion | flops 18874368 | bytes 28311556 | tf_op jit(solution)/shard_map/convert_element_type | solution.py:101
  600.5 4.9 all-to-all-start.1
  605.4 0.3 all-gather.2.cloned.1.call-start
  605.7 0.1 fusion.26
  605.8 0.1 broadcast_bitcast_fusion.1
  605.9 0.8 bitcast_multiply_fusion.1
  606.7 0.0 all-gather.2.cloned.1.call-update
  606.7 157.3 %all-gather.2.cloned.1.call-done = bf16[6144,256]{1,0:T(8,128)(2,1)} async-done(((bf16[384,256]{1,0:T(8,128)(2,1)}), bf16[6144,256]{1,0:T(8,128)(2,1)}) %all-gather.2.cloned.1.call-update) | async-done | bytes 3145744 | tf_op jit(solution)/shard_map/all_gather | solution.py:109
  764.0 1.5 collective-permute-start
  765.5 1.0 convolution_convert_fusion.2
  766.5 64.6 %all-to-all-done.1 = bf16[16,384,768]{2,1,0:T(8,128)(2,1)} async-done(((bf16[16,384,768]{2,1,0:T(8,128)(2,1)}), bf16[16,384,768]{2,1,0:T(8,128)(2,1)}, u32[]{:S(2)}, u32[]{:S(2)}) %all-to-all-start.1) | async-done | bytes 9437216 | tf_op jit(solution)/shard_map/all_to_all | solution.py:102
  831.1 12.2 %convert_bitcast_fusion = f32[16,48,8,768]{3,2,1,0:T(8,128)} fusion(bf16[16,384,768]{2,1,0:T(8,128)(2,1)} %all-to-all-done.1), kind=kLoop, calls=%fused_computation.3 | loop fusion | flops 4718592 | bytes 28311552
  843.3 12.9 %copy.14 = f32[16,48,8,768]{3,2,0,1:T(8,128)} copy(f32[16,48,8,768]{3,2,1,0:T(8,128)} %convert_bitcast_fusion) | data formatting | bytes 37748736 | tf_op jit(solution)/shard_map/convert_element_type | solution.py:117
  856.2 0.0 collective-permute-done
  856.2 20.5 %fusion.2 = bf16[1,384,12288]{2,1,0:T(8,128)(2,1)} fusion(f32[384,12288]{1,0:T(8,128)} %bitcast.59, bf16[384,256]{1,0:T(8,128)(2,1)} %convolution_convert_fusion.2, bf16[1,384,12288]{2,1,0:T(8,128)(2,1)} %param.16, bf16[6144,256]{1,0:T(8,128)(2,1)} %collective-permute-done, bf16[6144,256]{1,0:T(8,128)(2,1)S(1)} %copy-done.3, pred[]{:T(512)S(6)} %eq.35), kind=kOutput, calls=%fused_computation.5 | convolution fusion | flops 2463105024 | bytes 44236800 | tf_op jit(solution)/shard_map/dot_general | solution.py:40
  (28 shorter events, 0.3 us)
Async XLA Ops:
  6.5 9.0 %copy-start = (f32[1,256,256]{2,1,0:T(8,128)S(1)}, f32[1,256,256]{2,1,0:T(8,128)}, u32[]{:S(2)}) copy-start(f32[1,256,256]{2,1,0:T(8,128)} %param.10) | copy-start | bytes 786436
  9.3 10.5 %collective-permute-start.1 = (bf16[384,256]{1,0:T(8,128)(2,1)}, bf16[384,256]{1,0:T(8,128)(2,1)}, u32[]{:S(2)}, u32[]{:S(2)}) collective-permute-start(bf16[384,256]{1,0:T(8,128)(2,1)} %get-tuple-element.6), channel_id=1, source_target_pairs={{0,1},{1,2},{2,3},{3,4},{4,5},{5,6},{6,7},{7,8},{8,9},{9,10},{10,1... | collective-permute-start | bytes 589832 | tf_op jit(solution)/shard_map/ppermute | solution.py:77
  12.3 10.9 %collective-permute-start.2 = (bf16[384,256]{1,0:T(8,128)(2,1)}, bf16[384,256]{1,0:T(8,128)(2,1)}, u32[]{:S(2)}, u32[]{:S(2)}) collective-permute-start(bf16[384,256]{1,0:T(8,128)(2,1)} %get-tuple-element.6), channel_id=1, source_target_pairs={{0,15},{1,0},{2,1},{3,2},{4,3},{5,4},{6,5},{7,6},{8,7},{9,8},{10,9... | collective-permute-start | bytes 589832 | tf_op jit(solution)/shard_map/ppermute | solution.py:84
  14.7 76.3 %copy-start.2 = (bf16[1,384,6144]{2,1,0:T(8,128)(2,1)S(1)}, bf16[1,384,6144]{2,1,0:T(8,128)(2,1)}, u32[]{:S(2)}) copy-start(bf16[1,384,6144]{2,1,0:T(8,128)(2,1)} %param.11) | copy-start | bytes 14155780
  19.8 8.2 collective-permute-start.3
  23.2 10.6 %collective-permute-start.4 = (bf16[384,256]{1,0:T(8,128)(2,1)}, bf16[384,256]{1,0:T(8,128)(2,1)S(1)}, u32[]{:S(2)}, u32[]{:S(2)}) collective-permute-start(bf16[384,256]{1,0:T(8,128)(2,1)} %collective-permute-done.2), channel_id=1, source_target_pairs={{0,15},{1,0},{2,1},{3,2},{4,3},{5,4},{6,5},{7,6},{8,7},{9,8},{10,9... | collective-permute-start | bytes 589832 | tf_op jit(solution)/shard_map/ppermute | solution.py:84
  28.0 8.3 collective-permute-start.5
  33.9 10.7 %collective-permute-start.6 = (bf16[384,256]{1,0:T(8,128)(2,1)S(1)}, bf16[384,256]{1,0:T(8,128)(2,1)S(1)}, u32[]{:S(2)}, u32[]{:S(2)}) collective-permute-start(bf16[384,256]{1,0:T(8,128)(2,1)S(1)} %collective-permute-done.4), channel_id=1, source_target_pairs={{0,15},{1,0},{2,1},{3,2},{4,3},{5,4},{6,5},{7,6},{8,7},{9,8},{10,9... | collective-permute-start | bytes 589832 | tf_op jit(solution)/shard_map/ppermute | solution.py:84
  36.3 10.8 %collective-permute-start.7 = (bf16[384,256]{1,0:T(8,128)(2,1)S(1)}, bf16[384,256]{1,0:T(8,128)(2,1)S(1)}, u32[]{:S(2)}, u32[]{:S(2)}) collective-permute-start(bf16[384,256]{1,0:T(8,128)(2,1)S(1)} %collective-permute-done.5), channel_id=1, source_target_pairs={{0,1},{1,2},{2,3},{3,4},{4,5},{5,6},{6,7},{7,8},{8,9},{9,10},{10,1... | collective-permute-start | bytes 589832 | tf_op jit(solution)/shard_map/ppermute | solution.py:77
  44.6 11.1 %collective-permute-start.8 = (bf16[384,256]{1,0:T(8,128)(2,1)S(1)}, bf16[384,256]{1,0:T(8,128)(2,1)S(1)}, u32[]{:S(2)}, u32[]{:S(2)}) collective-permute-start(bf16[384,256]{1,0:T(8,128)(2,1)S(1)} %collective-permute-done.6), channel_id=1, source_target_pairs={{0,15},{1,0},{2,1},{3,2},{4,3},{5,4},{6,5},{7,6},{8,7},{9,8},{10,9... | collective-permute-start | bytes 589832 | tf_op jit(solution)/shard_map/ppermute | solution.py:84
  47.1 11.7 %collective-permute-start.9 = (bf16[384,256]{1,0:T(8,128)(2,1)S(1)}, bf16[384,256]{1,0:T(8,128)(2,1)S(1)}, u32[]{:S(2)}, u32[]{:S(2)}) collective-permute-start(bf16[384,256]{1,0:T(8,128)(2,1)S(1)} %collective-permute-done.7), channel_id=1, source_target_pairs={{0,1},{1,2},{2,3},{3,4},{4,5},{5,6},{6,7},{7,8},{8,9},{9,10},{10,1... | collective-permute-start | bytes 589832 | tf_op jit(solution)/shard_map/ppermute | solution.py:77
  55.7 11.1 %collective-permute-start.10 = (bf16[384,256]{1,0:T(8,128)(2,1)S(1)}, bf16[384,256]{1,0:T(8,128)(2,1)S(1)}, u32[]{:S(2)}, u32[]{:S(2)}) collective-permute-start(bf16[384,256]{1,0:T(8,128)(2,1)S(1)} %collective-permute-done.8), channel_id=1, source_target_pairs={{0,15},{1,0},{2,1},{3,2},{4,3},{5,4},{6,5},{7,6},{8,7},{9,8},{10,9... | collective-permute-start | bytes 589832 | tf_op jit(solution)/shard_map/ppermute | solution.py:84
  58.9 11.1 %collective-permute-start.11 = (bf16[384,256]{1,0:T(8,128)(2,1)S(1)}, bf16[384,256]{1,0:T(8,128)(2,1)S(1)}, u32[]{:S(2)}, u32[]{:S(2)}) collective-permute-start(bf16[384,256]{1,0:T(8,128)(2,1)S(1)} %collective-permute-done.9), channel_id=1, source_target_pairs={{0,1},{1,2},{2,3},{3,4},{4,5},{5,6},{6,7},{7,8},{8,9},{9,10},{10,1... | collective-permute-start | bytes 589832 | tf_op jit(solution)/shard_map/ppermute | solution.py:77
  66.8 10.3 %collective-permute-start.12 = (bf16[384,256]{1,0:T(8,128)(2,1)S(1)}, bf16[384,256]{1,0:T(8,128)(2,1)S(1)}, u32[]{:S(2)}, u32[]{:S(2)}) collective-permute-start(bf16[384,256]{1,0:T(8,128)(2,1)S(1)} %collective-permute-done.10), channel_id=1, source_target_pairs={{0,15},{1,0},{2,1},{3,2},{4,3},{5,4},{6,5},{7,6},{8,7},{9,8},{10,9... | collective-permute-start | bytes 589832 | tf_op jit(solution)/shard_map/ppermute | solution.py:84
  70.0 10.3 %collective-permute-start.13 = (bf16[384,256]{1,0:T(8,128)(2,1)S(1)}, bf16[384,256]{1,0:T(8,128)(2,1)S(1)}, u32[]{:S(2)}, u32[]{:S(2)}) collective-permute-start(bf16[384,256]{1,0:T(8,128)(2,1)S(1)} %collective-permute-done.11), channel_id=1, source_target_pairs={{0,1},{1,2},{2,3},{3,4},{4,5},{5,6},{6,7},{7,8},{8,9},{9,10},{10,1... | collective-permute-start | bytes 589832 | tf_op jit(solution)/shard_map/ppermute | solution.py:77
  77.1 10.7 %collective-permute-start.14 = (bf16[384,256]{1,0:T(8,128)(2,1)S(1)}, bf16[384,256]{1,0:T(8,128)(2,1)S(1)}, u32[]{:S(2)}, u32[]{:S(2)}) collective-permute-start(bf16[384,256]{1,0:T(8,128)(2,1)S(1)} %collective-permute-done.12), channel_id=1, source_target_pairs={{0,15},{1,0},{2,1},{3,2},{4,3},{5,4},{6,5},{7,6},{8,7},{9,8},{10,9... | collective-permute-start | bytes 589832 | tf_op jit(solution)/shard_map/ppermute | solution.py:84
  80.3 10.7 %collective-permute-start.15 = (bf16[384,256]{1,0:T(8,128)(2,1)S(1)}, bf16[384,256]{1,0:T(8,128)(2,1)S(1)}, u32[]{:S(2)}, u32[]{:S(2)}) collective-permute-start(bf16[384,256]{1,0:T(8,128)(2,1)S(1)} %collective-permute-done.13), channel_id=1, source_target_pairs={{0,1},{1,2},{2,3},{3,4},{4,5},{5,6},{6,7},{7,8},{8,9},{9,10},{10,1... | collective-permute-start | bytes 589832 | tf_op jit(solution)/shard_map/ppermute | solution.py:77
  126.6 213.2 %all-to-all-start = ((bf16[384,16,768]{2,0,1:T(8,128)(2,1)}), bf16[384,16,768]{2,0,1:T(8,128)(2,1)}, u32[]{:S(2)}, u32[]{:S(2)}) async-start(bf16[384,16,768]{2,0,1:T(8,128)(2,1)} %copy.10), calls=%async_computation | async-start | bytes 18874368 | tf_op jit(solution)/shard_map/all_to_all | solution.py:96
  383.7 204.8 %collective-permute-start.16 = (bf16[6144,768]{1,0:T(8,128)(2,1)}, bf16[6144,768]{1,0:T(8,128)(2,1)}, u32[]{:S(2)}, u32[]{:S(2)}) collective-permute-start(bf16[6144,768]{1,0:T(8,128)(2,1)} %constant_dynamic-slice_fusion), channel_id=1, source_target_pairs={{0,16},{16,0},{1,17},{17,1},{2,18},{18,2},{3,19},{19,3},{4,20},{20... | collective-permute-start | bytes 28311560 | tf_op jit(solution)/shard_map/ppermute | solution.py:10
  600.5 5.2 copy-start.6
  600.5 5.4 copy-start.4
  600.5 165.0 %copy-start.5 = (f32[1,256,256]{2,1,0:T(8,128)S(1)}, f32[1,256,256]{2,1,0:T(8,128)}, u32[]{:S(2)}) copy-start(f32[1,256,256]{2,1,0:T(8,128)} %param.15) | copy-start | bytes 786436
  600.5 230.6 %all-to-all-start.1 = ((bf16[16,384,768]{2,1,0:T(8,128)(2,1)}), bf16[16,384,768]{2,1,0:T(8,128)(2,1)}, u32[]{:S(2)}, u32[]{:S(2)}) async-start(bf16[16,384,768]{2,1,0:T(8,128)(2,1)} %bitcast.62), calls=%async_computation.1 | async-start | bytes 18874368 | tf_op jit(solution)/shard_map/all_to_all | solution.py:102
  605.4 158.6 %all-gather.2.cloned.1.call-start = ((), (), s32[]{:S(2)}) async-start(), calls=%async_computation.2 | async-start | bytes 3342336 | tf_op jit(solution)/shard_map/all_gather | solution.py:109
  764.0 92.2 %collective-permute-start = (bf16[6144,256]{1,0:T(8,128)(2,1)}, bf16[6144,256]{1,0:T(8,128)(2,1)}, u32[]{:S(2)}, u32[]{:S(2)}) collective-permute-start(bf16[6144,256]{1,0:T(8,128)(2,1)} %all-gather.2.cloned.1.call-done), channel_id=1, source_target_pairs={{0,16},{16,0},{1,17},{17,1},{2,18},{18,2},{3,19},{19,3},{4,20},{20... | collective-permute-start | bytes 9437192 | tf_op jit(solution)/shard_map/ppermute | solution.py:10
  843.3 12.9 %copy-start.3 = (bf16[6144,256]{1,0:T(8,128)(2,1)S(1)}, bf16[6144,256]{1,0:T(8,128)(2,1)}, u32[]{:S(2)}) copy-start(bf16[6144,256]{1,0:T(8,128)(2,1)} %all-gather.2.cloned.1.call-done) | copy-start | bytes 9437188
  856.2 20.5 %copy-start.1 = (f32[1,256,256]{2,1,0:T(8,128)S(1)}, f32[1,256,256]{2,1,0:T(8,128)}, u32[]{:S(2)}) copy-start(f32[1,256,256]{2,1,0:T(8,128)} %param.10) | copy-start | bytes 786436
Sparse Core Ops, SparseCore 0:
  608.6 155.3 all-gather.1
